TPU v7x, 32 devices: a whole 2x2x4 slice. The times are simulated.
32 devices in a mesh: member: 4 (over y, x), grid: 8 (over z, core).
Axes of the slice: x: 2, y: 2, z: 4, core: 2. Of those that a mesh axis runs over, the one named last changes fastest.
Arguments:
- latent: bfloat16 [4, 16384, 1024], P('member', 'grid'), may hold values from -6 to 6
- w_in: bfloat16 [1024, 1024], P(('member', 'grid')), may hold values from -0.1875 to 0.1875
- b_in: float32 [1024], replicated, may hold values from -3 to 3
- w_out: bfloat16 [100, 1024], replicated, may hold values from -0.1875 to 0.1875
- b_out: float32 [100], replicated, may hold values from -3 to 3
- targets: float32 [100, 16384], P(None, 'grid'), may hold values from -6 to 6
- var_weight: float32 [100], replicated, may hold values from 0.5 to 5
- plan: int32 [3, 4], replicated, may hold values from 0 to 3, as said below
Outputs:
- loss: float32 [], replicated
- grad_latent: bfloat16 [4, 16384, 1024], P('member', 'grid')
- grad_w_in: float32 [1024, 1024], P(('member', 'grid'))
- grad_b_in: float32 [1024], replicated
- grad_w_out: float32 [100, 1024], replicated
- grad_b_out: float32 [100], replicated
Inputs may be any that keep to these rules, and one draw needn't show every extreme that they name: `plan`: each row is a perfect pairing of the 4 members: no member is its own partner, the partner of a member's partner is the member, and no pair occurs in two rows.
All inputs are finite; a program needn't handle non-finite values.
Results may differ from a plain program's by a relative error of at most 0.0095.
Values may be sent and summed in bfloat16 or wider, within the bound.
A program may use at most 128 MiB of HBM per device.

v0:
```python
import functools
import math

import jax
import jax.numpy as jnp
from jax import lax
from jax.experimental import pallas as pl
from jax.experimental.pallas import tpu as pltpu
from jax.sharding import PartitionSpec as P

DELTA = 0.25


def make_fold(mine, partner_rows):

    def fold(carry, piece, start):
        count = piece.shape[0]
        labels = jnp.arange(count, dtype=jnp.int32)
        weights = jnp.sum((partner_rows[:, None] == labels[None, :]).astype(jnp.float32), axis=0)
        diff = mine[None] - piece
        root = jnp.sqrt(diff * diff + DELTA * DELTA)
        slope_sum = jnp.einsum("k,kvp->vp", weights, diff / root)
        spread_sum = jnp.einsum("k,kvp->vp", weights, root - DELTA)
        return (slope_sum, spread_sum)

    return fold


def shards(latent, w_in, b_in, w_out, b_out, targets, var_weight, plan):
    hidden_in = latent[0]
    points = hidden_in.shape[0]
    rounds = plan.shape[0]
    w_full = lax.all_gather(w_in, ("member", "grid"), axis=0, tiled=True)
    member = lax.axis_index("member")
    grid_index = lax.axis_index("grid")
    members = lax.axis_size("member")
    grid_count = lax.axis_size("grid")
    total = points * grid_count
    place = (grid_index * points + jnp.arange(points, dtype=jnp.int32)).astype(jnp.float32)
    area = jnp.cos(1.4 * (place + 0.5) / total)
    scale_map = area[None, :] * var_weight[:, None]
    partner_rows = lax.dynamic_index_in_dim(plan, member, 1, keepdims=False)
    pre = jnp.dot(hidden_in, w_full, preferred_element_type=jnp.float32) + b_in[None, :]
    act = jax.nn.gelu(pre).astype(jnp.bfloat16)
    field = jnp.dot(w_out, act.T, preferred_element_type=jnp.float32) + b_out[:, None]
    pre, act, field = (pre, act, field)
    fold_all = make_fold(field, partner_rows)
    slope_sum, spread_sum = fold_all(
        (
            jnp.zeros((w_out.shape[0], points), jnp.float32),
            jnp.zeros((w_out.shape[0], points), jnp.float32),
        ),
        lax.all_gather(field[None], "member", axis=0, tiled=True),
        jnp.int32(0),
    )
    miss = field - targets
    miss_root = jnp.sqrt(miss * miss + DELTA * DELTA)
    cot = scale_map * (miss / miss_root - slope_sum / rounds)
    terms = scale_map * (miss_root - DELTA - spread_sum / (2.0 * rounds))
    cot_b = cot.astype(jnp.bfloat16)
    dact = jnp.dot(cot_b.T, w_out, preferred_element_type=jnp.float32)
    _, pull = jax.vjp(jax.nn.gelu, pre)
    dpre = pull(dact)[0]
    dpre_b = dpre.astype(jnp.bfloat16)
    grad_hidden = jnp.dot(dpre_b, w_full.T, preferred_element_type=jnp.float32).astype(jnp.bfloat16)
    kappa = 4.0 / jnp.sqrt(jnp.float32(members * total))
    out_term = jnp.dot(cot_b, act, preferred_element_type=jnp.float32)
    sum_w2, sum_b2, sum_b1, sum_loss = lax.psum(
        (out_term, jnp.sum(cot, axis=1), jnp.sum(dpre, axis=0), jnp.sum(terms)), ("member", "grid")
    )
    row_count = w_in.shape[0]
    full_term = jnp.dot(hidden_in.T, dpre_b, preferred_element_type=jnp.float32)
    summed = lax.psum(full_term, ("member", "grid"))
    offset = (member * grid_count + grid_index) * row_count
    own_rows = lax.dynamic_slice_in_dim(summed, offset, row_count, 0)
    loss = sum_loss / (members * total * w_out.shape[0])
    return (
        loss,
        grad_hidden[None],
        own_rows * kappa,
        sum_b1 * kappa,
        sum_w2 * kappa,
        sum_b2 * kappa,
    )


TILE = 256
LANES = 128
BF = jnp.bfloat16
F32 = jnp.float32


def dot(a, b, dims):
    return lax.dot_general(a, b, (dims, ((), ())), preferred_element_type=F32)


NN = ((1,), (0,))
NT = ((1,), (1,))
TN = ((0,), (0,))


def head_kernel(
    members, planes, lat_hbm, w_in, b_in, w_out, b_out, tgt_hbm, vw,
    gh_hbm, g_w1, g_b1, g_w2, g_b2, g_loss,
    lat, lat_t, w_buf, gp, act, dpre, gh, fsend, frecv, csend, crecv, tgt, rowbuf, lane_sums,
    ot, op_send, op_recv, om_keep, om_send, om_recv, oz, w2, sm, sp_recv, smm, smz,
    keep, p_send, p_recv, m_send, m_recv, z_keep, z_send, z_recv,
    send_sem, recv_sem, local_sem, out_sem,
):
    m = lax.axis_index("member")
    g = lax.axis_index("grid")
    z, c = g // 2, lax.rem(g, 2)
    other = 1 - c
    points = lat.shape[1]
    width = lat.shape[2]
    sub = points // members
    rows = w_in.shape[0]
    vars_ = w_out.shape[0]
    latent = w_out.shape[1]
    total = points * planes * 2

    across, down = m + 1 - 2 * lax.rem(m, 2), m + 2 - 4 * (m // 2)
    order = (m, members - 1 - m, across, down)

    def mem(k):
        return order[k % members]

    def zed(k):
        return lax.rem(z + k + planes, planes)

    partner = (m, z * 2 + other)

    def member_dev(k):
        return (mem(k), g)

    def z_dev(k):
        return (m, zed(k) * 2 + c)

    started = []

    def send(src, dst, dev):
        n = len(started)
        copy = pltpu.make_async_remote_copy(
            src_ref=src, dst_ref=dst, send_sem=send_sem.at[n], recv_sem=recv_sem.at[n],
            device_id=dev, device_id_type=pl.DeviceIdType.MESH,
        )
        copy.start()
        started.append(copy)
        return copy

    loads = []
    for ch in range(members):
        copy = pltpu.make_async_copy(
            lat_hbm.at[0, :, pl.ds(ch * width, width)], lat.at[ch], local_sem.at[ch]
        )
        copy.start()
        loads.append(copy)
    own = pltpu.make_async_copy(w_in, w_buf.at[m, z, c], local_sem.at[members])
    own.start()
    tgt_copy = pltpu.make_async_copy(
        tgt_hbm.at[:, pl.ds(pl.multiple_of(m * sub, LANES), sub)], tgt, local_sem.at[members + 1]
    )
    tgt_copy.start()

    barrier = pltpu.get_barrier_semaphore()
    peers = [partner] + [z_dev(k) for k in range(1, planes)] + [member_dev(k) for k in range(1, members)]
    for dev in peers:
        pl.semaphore_signal(barrier, inc=1, device_id=dev, device_id_type=pl.DeviceIdType.MESH)
    pl.semaphore_wait(barrier, len(peers))

    z_copies = [None] + [send(w_in, w_buf.at[m, z, c], z_dev(k)) for k in range(1, planes)]
    own.wait()

    def transpose_chunk(ch):
        def body(t, carry):
            r0 = pl.multiple_of(t * TILE, TILE)
            lat_t[ch, :, pl.ds(r0, TILE)] = lat[ch, pl.ds(r0, TILE), :].T
            return carry
        lax.fori_loop(0, points // TILE, body, 0)

    rowbuf[...] = jnp.zeros_like(rowbuf)
    rowbuf[0:1, :vars_] = b_out[...]
    rowbuf[1:2, :vars_] = vw[...]
    b_col = jnp.broadcast_to(rowbuf[0:1, :], (LANES, LANES)).T[:vars_]
    v_col = jnp.broadcast_to(rowbuf[1:2, :], (LANES, LANES)).T[:vars_]
    lane_sums[...] = jnp.zeros_like(lane_sums)
    ot[...] = jnp.zeros_like(ot)
    sm[...] = jnp.zeros_like(sm)

    near = {2: [], 3: []}
    far = []
    to_part = {k: [] for k in range(members)}

    def hand_over(k, step):
        block = w_buf.at[mem(k), zed(-step), c]
        to_part[k].append(send(block, block, partner))
        return block

    def spread_block(step):
        if step > 0:
            z_copies[step].wait_recv()
        block = hand_over(0, step)
        for k in (2, 3):
            near[k].append(send(block, block, member_dev(k)))

    def relay_block(step):
        for k in (2, 3):
            near[k][step].wait_recv()
            block = hand_over(k, step)
            if step % 2 == k - 2:
                far.append(send(block, block, member_dev(5 - k)))

    def contract(k, first):
        ch = mem(k)
        for copy in to_part[k]:
            copy.wait_recv()

        def body(t, carry):
            r0 = pl.multiple_of(t * TILE, TILE)
            w = w_buf[ch].reshape(width, latent)
            before = b_in[...] if first else gp[pl.ds(r0, TILE), :]
            gp[pl.ds(r0, TILE), :] = before + dot(lat[ch, pl.ds(r0, TILE), :], w, NN)
            return carry

        lax.fori_loop(0, points // TILE, body, 0)

    for step in range(planes):
        spread_block(step)
        if step > 0:
            relay_block(step - 1)
        if step < members:
            loads[step].wait()
            transpose_chunk(step)
    for ch in range(planes, members):
        loads[ch].wait()
        transpose_chunk(ch)
    contract(0, True)
    relay_block(planes - 1)
    contract(2, False)
    contract(3, False)
    for step in range(planes):
        far[step].wait_recv()
        hand_over(1, step)
    for copy in to_part[1]:
        copy.wait_recv()

    last = mem(1)
    c0 = math.sqrt(2.0 / math.pi)
    parts = sub // TILE
    f_copies = {}
    for part in range(parts):
        for k in range(1, members + 1):
            r0 = pl.multiple_of(mem(k) * sub + part * TILE, TILE)
            x = dot(lat[last, pl.ds(r0, TILE), :], w_buf[last].reshape(width, latent), NN)
            x = x + gp[pl.ds(r0, TILE), :]
            sq = x * x
            cdf = 0.5 + 0.5 * jnp.tanh(x * (c0 + (0.044715 * c0) * sq))
            out = x * cdf
            act[pl.ds(r0, TILE), :] = out.astype(BF)
            gp[pl.ds(r0, TILE), :] = cdf + (out * (1.0 - cdf)) * (2.0 * c0 + (6.0 * 0.044715 * c0) * sq)
            field = dot(w_out[...], act[pl.ds(r0, TILE), :], NT)
            if k < members:
                fsend[part, k - 1] = field
                f_copies[part, k] = send(fsend.at[part, k - 1], frecv.at[part, k], member_dev(k))
            else:
                frecv[part, 0] = field

    tgt_copy.wait()
    eps = DELTA * DELTA
    b_sum = jnp.zeros((vars_, LANES), F32)
    l_sum = jnp.zeros((vars_, LANES), F32)
    c_copies = {}
    per_part = TILE // LANES
    for t in range(sub // LANES):
        part, at = t // per_part, t % per_part
        cols = slice(at * LANES, (at + 1) * LANES)
        if at == 0:
            for k in range(1, members):
                f_copies[part, k].wait_recv()
        place = lax.broadcasted_iota(jnp.int32, (1, LANES), 1) + (g * points + m * sub + t * LANES)
        area = jnp.cos(1.4 * (place.astype(F32) + 0.5) / total)
        scale = v_col * area
        f = [frecv[part, k, :, cols] for k in range(members)]
        goal = tgt[:, t * LANES:(t + 1) * LANES] - b_col
        pairs = [None] * members
        spread = jnp.zeros((vars_, LANES), F32)
        for a in range(members):
            for b in range(a + 1, members):
                d = f[a] - f[b]
                q = d * d + eps
                inv = lax.rsqrt(q)
                s = d * inv
                spread += q * inv - DELTA
                pairs[a] = s if pairs[a] is None else pairs[a] + s
                pairs[b] = -s if pairs[b] is None else pairs[b] - s
        miss_sum = jnp.zeros((vars_, LANES), F32)
        for a in range(members):
            d = f[a] - goal
            q = d * d + eps
            inv = lax.rsqrt(q)
            miss_sum += q * inv - DELTA
            cot = scale * (d * inv - pairs[a] * (1.0 / (members - 1)))
            b_sum += cot
            if a == 0:
                crecv[part, 0, :, cols] = cot.astype(BF)
            else:
                csend[part, a - 1, :, cols] = cot.astype(BF)
        l_sum += scale * (miss_sum - spread * (1.0 / (members - 1)))
        if at == per_part - 1:
            for a in range(1, members):
                c_copies[part, a] = send(csend.at[part, a - 1], crecv.at[part, a], member_dev(a))
    lane_sums[:vars_, :] = b_sum
    sm[1:2, :LANES] = jnp.sum(lane_sums[...].T, axis=0, keepdims=True)
    sm[1:2, LANES:2 * LANES] = jnp.sum(l_sum, axis=0, keepdims=True)

    col = jnp.zeros((1, latent), F32)
    for part, a in [(p, a) for p in range(parts) for a in range(members)]:
        if a > 0:
            c_copies[part, a].wait_recv()
        r0 = pl.multiple_of(mem(a) * sub + part * TILE, TILE)
        cot_b = crecv[part, a]
        d = dot(cot_b, w_out[...], TN) * gp[pl.ds(r0, TILE), :]
        dpre[pl.ds(r0, TILE), :] = d.astype(BF)
        ot[:vars_, :] += dot(cot_b, act[pl.ds(r0, TILE), :], NN)
        col += jnp.sum(d, axis=0, keepdims=True)
    sm[0:1, :] = col

    share = ot.shape[0] // (2 * members)
    first_half = pl.multiple_of(other * (members * share), share)
    op_send[...] = ot[pl.ds(first_half, members * share), :].astype(BF)
    op_copy = send(op_send, op_recv, partner)
    sp_copy = send(sm, sp_recv, partner)

    def chunk(k):
        t = mem(k)
        part = dot(lat_t[t], dpre[...], NN).reshape(planes, 2, rows, latent)
        gather_ref = keep
        gather_ref[...] = part
        p_send[k - 1] = keep[:, other].astype(BF)
        m_keep_k = keep[:, c]
        return m_keep_k, send(p_send.at[k - 1], p_recv.at[k - 1], partner)

    def chip_sum(k, mine, copy):
        copy.wait_recv()
        return mine + p_recv[k - 1].astype(F32)

    def to_member(k):
        p_copies[k].wait_recv()
        m_send[k - 1] = (z_keep[k - 1] + p_recv[k - 1].astype(F32)).astype(BF)
        m_copies[k] = [
            send(m_send.at[k - 1, zed(step)], m_recv.at[k - 1, zed(step)], member_dev(k))
            for step in list(range(1, planes)) + [0]
        ]

    p_copies = {}
    m_copies = {}

    def do_chunk(k):
        z_keep[k - 1], p_copies[k] = chunk(k)

    outs = []

    def hidden_grad(ch):
        def body(t, carry):
            r0 = pl.multiple_of(t * TILE, TILE)
            w = w_buf[ch].reshape(width, latent)
            gh[ch, pl.ds(r0, TILE), :] = dot(dpre[pl.ds(r0, TILE), :], w, NT).astype(BF)
            return carry

        lax.fori_loop(0, points // TILE, body, 0)
        copy = pltpu.make_async_copy(gh.at[ch], gh_hbm.at[0, :, pl.ds(ch * width, width)], out_sem.at[ch])
        copy.start()
        outs.append(copy)

    do_chunk(1)
    do_chunk(2)
    to_member(1)
    do_chunk(3)
    to_member(2)
    op_copy.wait_recv()
    mine = pl.multiple_of(c * (members * share), share)
    om_keep[...] = (ot[pl.ds(mine, members * share), :] + op_recv[...].astype(F32)).reshape(members, share, latent)
    om_send[...] = om_keep[...].astype(BF)
    om_copies = [send(om_send.at[mem(k)], om_recv.at[k - 1], member_dev(k)) for k in range(1, members)]
    sp_copy.wait_recv()
    smm[m] = sm[...] + sp_recv[...]
    sm_copies = [send(smm.at[m], smm.at[m], member_dev(k)) for k in range(1, members)]
    do_chunk(4)
    to_member(3)
    hidden_grad(0)
    acc = om_keep[m]
    for k in range(1, members):
        om_copies[k - 1].wait_recv()
        acc += om_recv[k - 1].astype(F32)
    oz[z] = acc.astype(BF)
    oz_copies = [send(oz.at[z], oz.at[z], z_dev(k)) for k in range(1, planes)]
    for copy in sm_copies:
        copy.wait_recv()
    acc = smm[0]
    for k in range(1, members):
        acc += smm[k]
    smz[z] = acc
    sz_copies = [send(smz.at[z], smz.at[z], z_dev(k)) for k in range(1, planes)]
    hidden_grad(1)
    for copy in oz_copies:
        copy.wait_recv()
    acc = oz[0].astype(F32)
    for k in range(1, planes):
        acc += oz[k].astype(F32)
    w2[c, m] = acc
    w2_copies = [send(w2.at[c, m], w2.at[c, m], member_dev(k)) for k in range(1, members)]
    hidden_grad(2)
    p_copies[members].wait_recv()

    def plane_sum(step):
        at = zed(step)
        acc = z_keep[members - 1, at] + p_recv[members - 1, at].astype(F32)
        for k in range(1, members):
            m_copies[k][(step - 1) % planes].wait_recv()
            acc += m_recv[k - 1, at].astype(F32)
        return acc

    zz_copies = []

    def to_plane(step):
        z_send[step] = plane_sum(step).astype(BF)
        zz_copies.append(send(z_send.at[step], z_recv.at[step - 1], z_dev(step)))

    to_plane(1)
    hidden_grad(3)
    for step in range(2, planes):
        to_plane(step)
    for copy in w2_copies:
        copy.wait_recv()
    half_copy = send(w2.at[c], w2.at[c], partner)
    z_keep[members - 1, z] = plane_sum(0)

    kappa = 4.0 / math.sqrt(members * total)
    for copy in sz_copies:
        copy.wait_recv()
    acc = smz[0]
    for k in range(1, planes):
        acc += smz[k]
    acc = acc * kappa
    g_b1[...] = acc[0:1, :]
    g_b2[...] = acc[1:2, :vars_]
    g_loss[...] = jnp.sum(acc[1:2, LANES:2 * LANES], axis=1, keepdims=True) * (1.0 / (kappa * members * total * vars_))
    half_copy.wait_recv()
    g_w2[...] = w2[...].reshape(2 * members * share, latent)[:vars_] * kappa

    acc = z_keep[members - 1, z]
    for k in range(1, planes):
        zz_copies[k - 1].wait_recv()
        acc += z_recv[k - 1].astype(F32)
    g_w1[...] = acc * kappa
    for copy in started:
        copy.wait_send()
    for copy in outs:
        copy.wait()


def fast(latent, w_in, b_in, w_out, b_out, targets, var_weight, plan):
    members = lax.axis_size("member")
    grid = lax.axis_size("grid")
    planes = grid // 2
    points, width = latent.shape[1], latent.shape[2]
    rows = w_in.shape[0]
    vars_ = w_out.shape[0]
    sub = points // members
    cw = width // members
    parts = sub // TILE
    share = 16 * pl.cdiv(vars_, 32 * members)
    n_sems = (planes - 1) * 4 + planes * 10 + (members - 1) * (3 + 2 * parts) + members + 3
    vmem = pl.BlockSpec(memory_space=pltpu.VMEM)
    hbm = pl.BlockSpec(memory_space=pl.ANY)
    V = pltpu.VMEM
    scratch = [
        V((members, points, cw), BF), V((members, cw, points), BF), V((members, planes, 2, rows, width), BF),
        V((points, width), F32), V((points, width), BF), V((points, width), BF), V((members, points, cw), BF),
        V((parts, members - 1, vars_, TILE), F32), V((parts, members, vars_, TILE), F32),
        V((parts, members - 1, vars_, TILE), BF), V((parts, members, vars_, TILE), BF), V((vars_, sub), F32),
        V((8, LANES), F32), V((LANES, LANES), F32),
        V((2 * members * share, width), F32), V((members * share, width), BF), V((members * share, width), BF),
        V((members, share, width), F32), V((members, share, width), BF), V((members - 1, share, width), BF),
        V((planes, share, width), BF), V((2, members, share, width), F32),
        V((2, width), F32), V((2, width), F32), V((members, 2, width), F32), V((planes, 2, width), F32),
        V((planes, 2, rows, width), F32), V((members, planes, rows, width), BF), V((members, planes, rows, width), BF),
        V((members - 1, planes, rows, width), BF), V((members - 1, planes, rows, width), BF),
        V((members, planes, rows, width), F32), V((planes, rows, width), BF), V((planes - 1, rows, width), BF),
        pltpu.SemaphoreType.DMA((n_sems,)), pltpu.SemaphoreType.DMA((n_sems,)),
        pltpu.SemaphoreType.DMA((members + 2,)), pltpu.SemaphoreType.DMA((members,)),
    ]
    S = jax.ShapeDtypeStruct
    gh, g_w1, g_b1, g_w2, g_b2, g_loss = pl.pallas_call(
        functools.partial(head_kernel, members, planes),
        out_shape=[
            S((1, points, width), BF), S((rows, width), F32), S((1, width), F32),
            S((vars_, width), F32), S((1, vars_), F32), S((1, 1), F32),
        ],
        in_specs=[hbm, vmem, vmem, vmem, vmem, hbm, vmem],
        out_specs=[hbm, vmem, vmem, vmem, vmem, vmem],
        scratch_shapes=scratch,
        compiler_params=pltpu.CompilerParams(
            collective_id=0, has_side_effects=True, vmem_limit_bytes=60 * 1024 * 1024
        ),
    )(latent, w_in, b_in[None], w_out, b_out[None], targets, var_weight[None])
    return g_loss[0, 0], gh, g_w1, g_b1[0], g_w2, g_b2[0]


def local(latent, w_in, b_in, w_out, b_out, targets, var_weight, plan):
    members = lax.axis_size("member")
    grid = lax.axis_size("grid")
    points, width = latent.shape[1], latent.shape[2]
    whole_plan = plan.shape[0] == members - 1
    tiled = (
        w_in.shape[0] % 16 == 0 and grid % 2 == 0 and grid >= 4 and members == 4
        and points % (members * TILE) == 0 and width % (members * LANES) == 0
        and width // members == grid * w_in.shape[0] and w_out.shape[0] <= LANES
        and points * width <= 2048 * 1024
    )
    run = fast if whole_plan and tiled else shards
    return run(latent, w_in, b_in, w_out, b_out, targets, var_weight, plan)


def solution(mesh):
    placed = (
        P("member", "grid", None),
        P(("member", "grid"), None),
        P(),
        P(),
        P(),
        P(None, "grid"),
        P(),
        P(),
    )
    return jax.shard_map(
        local,
        mesh=mesh,
        in_specs=placed,
        out_specs=(P(), P("member", "grid", None), P(("member", "grid"), None), P(), P(), P()),
        check_vma=False,
    )
```

profile of v0, /device:TPU:0, one launch (start us, length us, event | category | flops | bytes accessed | tf_op | source)
XLA Modules:
  0.0 90.4 jit_solution(6298862585477754821)
XLA Ops:
  0.6 80.7 %shard_map.118 = (bf16[1,2048,1024]{2,1,0:T(8,128)(2,1)}, f32[32,1024]{1,0:T(8,128)}, f32[1,1024]{1,0:T(1,128)}, f32[100,1024]{1,0:T(8,128)}, f32[1,100]{1,0:T(1,128)}, /*index=5*/f32[1,1]{1,0:T(1,128)}) custom-call(bf16[1,2048,1024]{2,1,0:T(8,128)(2,1)} %lat_hbm.1, bf16[32,1024]{1,0:T(8,128)(2,1)} %w_in.1, f32[1,1024]{1,0:T(1,128)} %bitcast.6, ...), custom_call_target="tpu_custom_call" | custom-call | tf_op jit(solution)/shard_map/pallas_call | solution.py:494
  82.0 0.0 copy-start.1
  82.0 0.0 copy-start.2
  82.0 0.0 copy-start
  82.0 0.0 copy-start.3
  82.0 4.7 %copy.20 = bf16[1,2048,1024]{2,1,0:T(8,128)(2,1)} copy(bf16[1,2048,1024]{2,1,0:T(8,128)(2,1)} %get-tuple-element.25) | data formatting | bytes 8388608
  86.7 0.0 copy-done.1
  86.7 0.7 copy.21
  87.4 0.0 copy-done.2
  87.4 0.6 copy.22
  88.0 0.0 copy-done
  88.0 0.8 copy.23
  88.8 0.0 copy-done.3
  88.8 0.5 copy.24
Async XLA Ops:
  82.0 4.7 %copy-start.1 = (f32[32,1024]{1,0:T(8,128)S(1)}, f32[32,1024]{1,0:T(8,128)}, u32[]{:S(2)}) copy-start(f32[32,1024]{1,0:T(8,128)} %get-tuple-element.26) | copy-start | bytes 393220
  82.0 5.4 %copy-start.2 = (f32[1,1024]{1,0:T(1,128)S(1)}, f32[1,1024]{1,0:T(1,128)}, u32[]{:S(2)}) copy-start(f32[1,1024]{1,0:T(1,128)} %get-tuple-element.15) | copy-start | bytes 12292
  82.0 6.0 %copy-start = (f32[100,1024]{1,0:T(8,128)S(1)}, f32[100,1024]{1,0:T(8,128)}, u32[]{:S(2)}) copy-start(f32[100,1024]{1,0:T(8,128)} %get-tuple-element.28) | copy-start | bytes 1228804
  82.0 6.7 %copy-start.3 = (f32[1,100]{1,0:T(1,128)S(1)}, f32[1,100]{1,0:T(1,128)}, u32[]{:S(2)}) copy-start(f32[1,100]{1,0:T(1,128)} %get-tuple-element.17) | copy-start | bytes 1204
where the time goes:
time: 90.6 us; the launch traced here: 90.4 us
  Pallas kernels  80.7 us (89%)
  local copies, waits for them, and re-layouts  7.23 us (8%)
  between operations  2.5 us (3%)
    pallas_call x1, Pallas kernels, fast(): pl.pallas_call(functools.partial(head_kernel, members, planes), out_shape...  80.7 us
    unnamed x13, local copies, waits for them, and re-layouts  7.23 us

commit v1 on v0

v1 whole, which is shorter than its diff:
```python
import functools
import math

import jax
import jax.numpy as jnp
from jax import lax
from jax.experimental import pallas as pl
from jax.experimental.pallas import tpu as pltpu
from jax.sharding import PartitionSpec as P

DELTA = 0.25


def make_fold(mine, partner_rows):

    def fold(carry, piece, start):
        count = piece.shape[0]
        labels = jnp.arange(count, dtype=jnp.int32)
        weights = jnp.sum((partner_rows[:, None] == labels[None, :]).astype(jnp.float32), axis=0)
        diff = mine[None] - piece
        root = jnp.sqrt(diff * diff + DELTA * DELTA)
        slope_sum = jnp.einsum("k,kvp->vp", weights, diff / root)
        spread_sum = jnp.einsum("k,kvp->vp", weights, root - DELTA)
        return (slope_sum, spread_sum)

    return fold


def shards(latent, w_in, b_in, w_out, b_out, targets, var_weight, plan):
    hidden_in = latent[0]
    points = hidden_in.shape[0]
    rounds = plan.shape[0]
    w_full = lax.all_gather(w_in, ("member", "grid"), axis=0, tiled=True)
    member = lax.axis_index("member")
    grid_index = lax.axis_index("grid")
    members = lax.axis_size("member")
    grid_count = lax.axis_size("grid")
    total = points * grid_count
    place = (grid_index * points + jnp.arange(points, dtype=jnp.int32)).astype(jnp.float32)
    area = jnp.cos(1.4 * (place + 0.5) / total)
    scale_map = area[None, :] * var_weight[:, None]
    partner_rows = lax.dynamic_index_in_dim(plan, member, 1, keepdims=False)
    pre = jnp.dot(hidden_in, w_full, preferred_element_type=jnp.float32) + b_in[None, :]
    act = jax.nn.gelu(pre).astype(jnp.bfloat16)
    field = jnp.dot(w_out, act.T, preferred_element_type=jnp.float32) + b_out[:, None]
    pre, act, field = (pre, act, field)
    fold_all = make_fold(field, partner_rows)
    slope_sum, spread_sum = fold_all(
        (
            jnp.zeros((w_out.shape[0], points), jnp.float32),
            jnp.zeros((w_out.shape[0], points), jnp.float32),
        ),
        lax.all_gather(field[None], "member", axis=0, tiled=True),
        jnp.int32(0),
    )
    miss = field - targets
    miss_root = jnp.sqrt(miss * miss + DELTA * DELTA)
    cot = scale_map * (miss / miss_root - slope_sum / rounds)
    terms = scale_map * (miss_root - DELTA - spread_sum / (2.0 * rounds))
    cot_b = cot.astype(jnp.bfloat16)
    dact = jnp.dot(cot_b.T, w_out, preferred_element_type=jnp.float32)
    _, pull = jax.vjp(jax.nn.gelu, pre)
    dpre = pull(dact)[0]
    dpre_b = dpre.astype(jnp.bfloat16)
    grad_hidden = jnp.dot(dpre_b, w_full.T, preferred_element_type=jnp.float32).astype(jnp.bfloat16)
    kappa = 4.0 / jnp.sqrt(jnp.float32(members * total))
    out_term = jnp.dot(cot_b, act, preferred_element_type=jnp.float32)
    sum_w2, sum_b2, sum_b1, sum_loss = lax.psum(
        (out_term, jnp.sum(cot, axis=1), jnp.sum(dpre, axis=0), jnp.sum(terms)), ("member", "grid")
    )
    row_count = w_in.shape[0]
    full_term = jnp.dot(hidden_in.T, dpre_b, preferred_element_type=jnp.float32)
    summed = lax.psum(full_term, ("member", "grid"))
    offset = (member * grid_count + grid_index) * row_count
    own_rows = lax.dynamic_slice_in_dim(summed, offset, row_count, 0)
    loss = sum_loss / (members * total * w_out.shape[0])
    return (
        loss,
        grad_hidden[None],
        own_rows * kappa,
        sum_b1 * kappa,
        sum_w2 * kappa,
        sum_b2 * kappa,
    )


TILE = 256
LANES = 128
BF = jnp.bfloat16
F32 = jnp.float32
I16 = jnp.int16
TOP = 32767.0
DIAG, ACROSS, DOWN, SELF = 0, 1, 2, 3


def dot(a, b, dims):
    return lax.dot_general(a, b, (dims, ((), ())), preferred_element_type=F32)


NN = ((1,), (0,))
NT = ((1,), (1,))
TN = ((0,), (0,))


def head_kernel(
    members, planes, lat_hbm, w_in, b_in, w_out, b_out, tgt_hbm, vw,
    gh, g_w1, g_b1, g_w2, g_b2, g_loss,
    lat, lat_t, w_buf, gp, act, dpre, wo, fown, fsend, frecv, csend, crecv, tgt, rowbuf, lane_sums,
    ot, op_send, op_recv, om, om_send, om_recv, oq, w2, sm, sp_recv, smm, smz,
    keep, part_sum, p_send, p_recv, d_send, d_recv, n_send, n_recv, z_send, z_recv,
    send_sem, recv_sem, local_sem,
):
    m = lax.axis_index("member")
    g = lax.axis_index("grid")
    z, c = g // 2, lax.rem(g, 2)
    other = 1 - c
    points = lat.shape[1]
    width = lat.shape[2]
    sub = points // members
    rows = w_in.shape[0]
    vars_ = w_out.shape[0]
    pad = wo.shape[0]
    latent = w_out.shape[1]
    total = points * planes * 2
    half = width // 2

    mem = (members - 1 - m, m + 1 - 2 * lax.rem(m, 2), m + 2 - 4 * (m // 2), m)
    zed = (z, z + 1 - 2 * lax.rem(z, 2), z + 2 - 4 * (z // 2), planes - 1 - z)

    partner = (m, z * 2 + other)

    def member_dev(s):
        return (mem[s], g)

    def z_dev(k):
        return (m, zed[k] * 2 + c)

    started = []

    def send(src, dst, dev):
        n = len(started)
        copy = pltpu.make_async_remote_copy(
            src_ref=src, dst_ref=dst, send_sem=send_sem.at[n], recv_sem=recv_sem.at[n],
            device_id=dev, device_id_type=pl.DeviceIdType.MESH,
        )
        copy.start()
        started.append(copy)
        return copy

    loads = []
    for s in (SELF, ACROSS, DOWN, DIAG):
        copy = pltpu.make_async_copy(
            lat_hbm.at[0, :, pl.ds(pl.multiple_of(mem[s] * width, LANES), width)], lat.at[s], local_sem.at[s]
        )
        copy.start()
        loads.append((s, copy))
    own = pltpu.make_async_copy(w_in, w_buf.at[m, z, c], local_sem.at[members])
    own.start()
    tgt_copy = pltpu.make_async_copy(
        tgt_hbm.at[:, pl.ds(pl.multiple_of(m * sub, LANES), sub)], tgt, local_sem.at[members + 1]
    )
    tgt_copy.start()

    barrier = pltpu.get_barrier_semaphore()
    peers = [partner] + [z_dev(k) for k in range(1, planes)] + [member_dev(s) for s in (DIAG, ACROSS, DOWN)]
    for dev in peers:
        pl.semaphore_signal(barrier, inc=1, device_id=dev, device_id_type=pl.DeviceIdType.MESH)
    pl.semaphore_wait(barrier, len(peers))

    near = {ACROSS: [], DOWN: []}
    far = []
    to_part = {s: [] for s in range(members)}
    z_copies = [None]

    def block(s, step):
        return w_buf.at[mem[s], zed[step], c]

    def hand_over(s, step):
        to_part[s].append(send(block(s, step), block(s, step), partner))

    def spread_block(step):
        if step > 0:
            z_copies[step].wait_recv()
        src = w_in if step == 0 else block(SELF, step)
        for s in (ACROSS, DOWN):
            near[s].append(send(src, block(SELF, step), member_dev(s)))
        to_part[SELF].append(send(src, block(SELF, step), partner))

    def relay_block(step):
        for s in (ACROSS, DOWN):
            near[s][step].wait_recv()
        s = ACROSS if step % 2 == 0 else DOWN
        far.append(send(block(s, step), block(s, step), member_dev(ACROSS + DOWN - s)))
        hand_over(ACROSS, step)
        hand_over(DOWN, step)

    def far_block(step):
        far[step].wait_recv()
        hand_over(DIAG, step)

    def transpose_next():
        s, copy = loads.pop(0)
        copy.wait()

        def body(t, carry):
            r0 = pl.multiple_of(t * 2 * TILE, 2 * TILE)
            turned = lat[s, pl.ds(r0, 2 * TILE), :].T
            lat_t[0, s, :, pl.ds(r0, 2 * TILE)] = turned[:half]
            lat_t[1, s, :, pl.ds(r0, 2 * TILE)] = turned[half:]
            return carry

        lax.fori_loop(0, points // (2 * TILE), body, 0)

    def contract(slots, first):
        for s in slots:
            for copy in to_part[s]:
                copy.wait_recv()
        big = 4 * TILE

        def body(t, carry):
            r0 = pl.multiple_of(t * big, big)
            acc = b_in[...] if first else gp[pl.ds(r0, big), :]
            for s in slots:
                acc = acc + dot(lat[s, pl.ds(r0, big), :], w_buf[mem[s]].reshape(width, latent), NN)
            gp[pl.ds(r0, big), :] = acc
            return carry

        lax.fori_loop(0, points // big, body, 0)

    for k in range(1, planes):
        z_copies.append(send(w_in, w_buf.at[m, z, c], z_dev(k)))
    spread_block(0)

    wo[...] = jnp.zeros_like(wo)
    wo[:vars_, :] = w_out[...]
    rowbuf[...] = jnp.zeros_like(rowbuf)
    rowbuf[0:1, :vars_] = b_out[...]
    rowbuf[1:2, :vars_] = vw[...]
    b_col = jnp.broadcast_to(rowbuf[0:1, :], (LANES, LANES)).T[:vars_]
    v_col = jnp.broadcast_to(rowbuf[1:2, :], (LANES, LANES)).T[:vars_]
    lane_sums[...] = jnp.zeros_like(lane_sums)
    ot[...] = jnp.zeros_like(ot)
    sm[...] = jnp.zeros_like(sm)
    own.wait()

    transpose_next()
    relay_block(0)
    spread_block(1)
    transpose_next()
    spread_block(2)
    relay_block(1)
    transpose_next()
    spread_block(3)
    relay_block(2)
    far_block(0)
    transpose_next()
    contract((SELF,), True)
    relay_block(3)
    far_block(1)
    far_block(2)
    contract((ACROSS, DOWN), False)
    far_block(3)
    for copy in to_part[DIAG]:
        copy.wait_recv()

    c0 = math.sqrt(2.0 / math.pi)
    parts = sub // TILE
    f_copies = {}
    eps = DELTA * DELTA
    c_copies = {}
    sums = {"b": jnp.zeros((vars_, LANES), F32), "l": jnp.zeros((vars_, LANES), F32)}

    def forward_tile(part, s):
        r0 = pl.multiple_of(mem[s] * sub + part * TILE, TILE)
        x = dot(lat[DIAG, pl.ds(r0, TILE), :], w_buf[mem[DIAG]].reshape(width, latent), NN)
        x = x + gp[pl.ds(r0, TILE), :]
        sq = x * x
        cdf = 0.5 + 0.5 * jnp.tanh(x * (c0 + (0.044715 * c0) * sq))
        out = x * cdf
        act[pl.ds(r0, TILE), :] = out.astype(BF)
        gp[pl.ds(r0, TILE), :] = cdf + (out * (1.0 - cdf)) * (2.0 * c0 + (6.0 * 0.044715 * c0) * sq)
        field = dot(wo[...], act[pl.ds(r0, TILE), :], NT)
        if s == SELF:
            fown[part] = field[:vars_]
        else:
            peak = jnp.max(jnp.abs(field), axis=0, keepdims=True)
            code = jnp.floor(jnp.sqrt(peak) * 64.0) + 2.0
            scale = (code * code) * (1.0 / 4096.0)
            coded = jnp.round(field * (TOP / scale))
            at = lax.broadcasted_iota(jnp.int32, (pad, TILE), 0)
            coded = jnp.where(at == vars_, jnp.broadcast_to(code, (pad, TILE)), coded)
            fsend[part, s] = coded.astype(jnp.int32).astype(I16)
            f_copies[part, s] = send(fsend.at[part, s], frecv.at[part, s], member_dev(s))

    def score(part):
        for s in (DIAG, ACROSS, DOWN):
            f_copies[part, s].wait_recv()
        b_sum, l_sum = sums["b"], sums["l"]
        for at in range(TILE // LANES):
            cols = slice(at * LANES, (at + 1) * LANES)
            first = part * TILE + at * LANES
            place = lax.broadcasted_iota(jnp.int32, (1, LANES), 1) + (g * points + m * sub + first)
            area = jnp.cos(1.4 * (place.astype(F32) + 0.5) / total)
            scale = v_col * area
            f = []
            for s in (DIAG, ACROSS, DOWN):
                coded = frecv[part, s, :, cols].astype(jnp.int32).astype(F32)
                code = coded[vars_:vars_ + 1]
                f.append(coded[:vars_] * ((code * code) * (1.0 / (4096.0 * TOP))))
            f.append(fown[part, :, cols])
            goal = tgt[:, first:first + LANES] - b_col
            pairs = [None] * members
            spread = jnp.zeros((vars_, LANES), F32)
            for i in range(members):
                for j in range(i + 1, members):
                    d = f[i] - f[j]
                    q = d * d + eps
                    inv = lax.rsqrt(q)
                    slope = d * inv
                    spread += q * inv - DELTA
                    pairs[i] = slope if pairs[i] is None else pairs[i] + slope
                    pairs[j] = -slope if pairs[j] is None else pairs[j] - slope
            miss_sum = jnp.zeros((vars_, LANES), F32)
            for s in range(members):
                d = f[s] - goal
                q = d * d + eps
                inv = lax.rsqrt(q)
                miss_sum += q * inv - DELTA
                cot = scale * (d * inv - pairs[s] * (1.0 / (members - 1)))
                b_sum += cot
                if s == SELF:
                    crecv[part, SELF, :, cols] = cot.astype(BF)
                else:
                    csend[part, s, :, cols] = cot.astype(BF)
            l_sum += scale * (miss_sum - spread * (1.0 / (members - 1)))
        sums["b"], sums["l"] = b_sum, l_sum
        for s in (DIAG, ACROSS, DOWN):
            c_copies[part, s] = send(csend.at[part, s], crecv.at[part, s], member_dev(s))

    tgt_copy.wait()
    for part in range(parts):
        for s in (DIAG, ACROSS, DOWN):
            forward_tile(part, s)
        if part > 0:
            score(part - 1)
        forward_tile(part, SELF)
    score(parts - 1)
    lane_sums[:vars_, :] = sums["b"]
    sm[1:2, :LANES] = jnp.sum(lane_sums[...].T, axis=0, keepdims=True)
    sm[1:2, LANES:2 * LANES] = jnp.sum(sums["l"], axis=0, keepdims=True)

    col = jnp.zeros((1, latent), F32)
    for part in range(parts):
        for s in (SELF, ACROSS, DOWN, DIAG):
            if s != SELF:
                c_copies[part, s].wait_recv()
            r0 = pl.multiple_of(mem[s] * sub + part * TILE, TILE)
            cot_b = crecv[part, s]
            d = dot(cot_b, w_out[...], TN) * gp[pl.ds(r0, TILE), :]
            dpre[pl.ds(r0, TILE), :] = d.astype(BF)
            ot[:vars_, :] += dot(cot_b, act[pl.ds(r0, TILE), :], NN)
            col += jnp.sum(d, axis=0, keepdims=True)
    sm[0:1, :] = col

    share = ot.shape[0] // (2 * planes)
    first_half = pl.multiple_of(other * (planes * share), share)
    op_send[...] = ot[pl.ds(first_half, planes * share), :].astype(BF)
    op_copy = send(op_send, op_recv, partner)
    sp_copy = send(sm, sp_recv, partner)

    p_copies = {}
    d_copies = {}
    n_copies = {}
    far_half = 1 - z // 2
    halves = (far_half, z // 2)
    pairs_of = ((DIAG, ACROSS), (DOWN, SELF))

    def chunk(h, pair):
        n = h * 2 + pair
        lo = pair * 2
        left = lat_t[halves[h], lo:lo + 2].reshape(width, points)
        keep[...] = dot(left, dpre[...], NN).reshape(2, 2, 2, rows, latent)
        p_send[n] = keep[:, :, other].astype(BF)
        part_sum[h, lo:lo + 2] = keep[:, :, c]
        p_copies[n] = send(p_send.at[n], p_recv.at[n], partner)

    def fold(h, pair):
        n = h * 2 + pair
        p_copies[n].wait_recv()
        lo = pair * 2
        both = part_sum[h, lo:lo + 2] + p_recv[n].astype(F32)
        if pair == 0:
            d_send[h] = both[0].astype(BF)
            d_copies[h] = [
                send(d_send.at[h, j], d_recv.at[h, j], member_dev(ACROSS + j)) for j in range(2)
            ]
            n_send[h, 0, 0] = both[1, 0].astype(BF)
            n_copies[h, ACROSS, 0] = send(n_send.at[h, 0, 0], n_recv.at[h, 0, 0], member_dev(ACROSS))
            part_sum[h, ACROSS, 1] = both[1, 1]
        else:
            n_send[h, 1, 1] = both[0, 1].astype(BF)
            n_copies[h, DOWN, 1] = send(n_send.at[h, 1, 1], n_recv.at[h, 1, 1], member_dev(DOWN))
            part_sum[h, DOWN, 0] = both[0, 0]
            part_sum[h, SELF] = both[1]

    def relay_sum(h):
        for s, j in ((DOWN, 0), (ACROSS, 1)):
            d_copies[h][j].wait_recv()
            n_send[h, s - 1, j] = (part_sum[h, s, j] + d_recv[h, j].astype(F32)).astype(BF)
            n_copies[h, s, j] = send(n_send.at[h, s - 1, j], n_recv.at[h, s - 1, j], member_dev(s))

    def plane_sum(h):
        for s in (ACROSS, DOWN):
            for j in range(2):
                n_copies[h, s, j].wait_recv()
        part_sum[h, SELF] = (part_sum[h, SELF] + n_recv[h, 0].astype(F32)) + n_recv[h, 1].astype(F32)

    side = lax.rem(z, 2)
    zz_copies = {}

    def to_plane(k):
        h = 0 if k > 1 else 1
        j = side if k == 2 else 1 - side
        z_send[k - 1] = part_sum[h, SELF, j].astype(BF)
        zz_copies[k] = send(z_send.at[k - 1], z_recv.at[k - 1], z_dev(k))

    def hidden_grad(ch):
        w = w_buf[ch].reshape(width, latent)
        gh[0, :, ch * width:(ch + 1) * width] = dot(dpre[...], w, NT).astype(BF)

    chunk(0, 0)
    chunk(0, 1)
    fold(0, 0)
    chunk(1, 0)
    fold(0, 1)
    op_copy.wait_recv()
    mine = pl.multiple_of(c * (planes * share), share)
    om[...] = (ot[pl.ds(mine, planes * share), :] + op_recv[...].astype(F32)).reshape(planes, share, latent)
    om_send[...] = om[...].astype(BF)
    om_copies = [send(om_send.at[zed[k]], om_recv.at[k - 1], z_dev(k)) for k in range(1, planes)]
    sp_copy.wait_recv()
    smm[m] = sm[...] + sp_recv[...]
    sm_copies = [send(smm.at[m], smm.at[m], member_dev(s)) for s in (DIAG, ACROSS, DOWN)]
    chunk(1, 1)
    relay_sum(0)
    fold(1, 0)
    fold(1, 1)
    hidden_grad(0)
    acc = om[z]
    for k in range(1, planes):
        om_copies[k - 1].wait_recv()
        acc += om_recv[k - 1].astype(F32)
    oq[m] = acc.astype(BF)
    oq_copies = [send(oq.at[m], oq.at[m], member_dev(s)) for s in (DIAG, ACROSS, DOWN)]
    for copy in sm_copies:
        copy.wait_recv()
    acc = smm[0]
    for k in range(1, members):
        acc += smm[k]
    smz[z] = acc
    sz_copies = [send(smz.at[z], smz.at[z], z_dev(k)) for k in range(1, planes)]
    plane_sum(0)
    to_plane(2)
    to_plane(3)
    hidden_grad(1)
    relay_sum(1)
    hidden_grad(2)
    for copy in oq_copies:
        copy.wait_recv()
    acc = oq[0].astype(F32)
    for k in range(1, members):
        acc += oq[k].astype(F32)
    w2[c, z] = acc.astype(BF)
    w2_copies = [send(w2.at[c, z], w2.at[c, z], z_dev(k)) for k in range(1, planes)]
    hidden_grad(3)
    plane_sum(1)
    to_plane(1)
    part_sum[1, SELF, 0] = part_sum[1, SELF, side]

    kappa = 4.0 / math.sqrt(members * total)
    for copy in sz_copies:
        copy.wait_recv()
    acc = smz[0]
    for k in range(1, planes):
        acc += smz[k]
    acc = acc * kappa
    g_b1[...] = acc[0:1, :]
    g_b2[...] = acc[1:2, :vars_]
    g_loss[...] = jnp.sum(acc[1:2, LANES:2 * LANES], axis=1, keepdims=True) * (1.0 / (kappa * members * total * vars_))
    for copy in w2_copies:
        copy.wait_recv()
    half_copy = send(w2.at[c], w2.at[c], partner)

    acc = part_sum[1, SELF, 0]
    for k in (2, 3, 1):
        zz_copies[k].wait_recv()
        acc += z_recv[k - 1].astype(F32)
    g_w1[...] = acc * kappa
    half_copy.wait_recv()
    g_w2[...] = w2[...].reshape(2 * planes * share, latent)[:vars_].astype(F32) * kappa
    for copy in started:
        copy.wait_send()


def store_kernel(*refs):
    count = len(refs) // 2
    copies = []
    for n in range(count):
        copy = pltpu.make_async_copy(refs[n], refs[count + n], refs[2 * count].at[n])
        copy.start()
        copies.append(copy)
    for copy in copies:
        copy.wait()


def fast(latent, w_in, b_in, w_out, b_out, targets, var_weight, plan):
    members = lax.axis_size("member")
    grid = lax.axis_size("grid")
    planes = grid // 2
    points, width = latent.shape[1], latent.shape[2]
    rows = w_in.shape[0]
    vars_ = w_out.shape[0]
    sub = points // members
    cw = width // members
    parts = sub // TILE
    share = 16 * pl.cdiv(vars_, 32 * planes)
    pad = 8 * pl.cdiv(vars_ + 1, 8)
    n_sems = (planes - 1) * 4 + planes * 10 + (members - 1) * (4 + 2 * parts) + 2 * members + 24
    vmem = pl.BlockSpec(memory_space=pltpu.VMEM)
    hbm = pl.BlockSpec(memory_space=pl.ANY)
    V = pltpu.VMEM
    block = (rows, width)
    scratch = [
        V((members, points, cw), BF), V((2, members, cw // 2, points), BF), V((members, planes, 2, *block), BF),
        V((points, width), F32), V((points, width), BF), V((points, width), BF),
        V((pad, width), BF), V((parts, vars_, TILE), F32),
        V((parts, members - 1, pad, TILE), I16), V((parts, members - 1, pad, TILE), I16),
        V((parts, members - 1, vars_, TILE), BF), V((parts, members, vars_, TILE), BF), V((vars_, sub), F32),
        V((8, LANES), F32), V((LANES, LANES), F32),
        V((2 * planes * share, width), F32), V((planes * share, width), BF), V((planes * share, width), BF),
        V((planes, share, width), F32), V((planes, share, width), BF), V((planes - 1, share, width), BF),
        V((members, share, width), BF), V((2, planes, share, width), BF),
        V((2, width), F32), V((2, width), F32), V((members, 2, width), F32), V((planes, 2, width), F32),
        V((2, 2, 2, *block), F32), V((2, members, 2, *block), F32),
        V((4, 2, 2, *block), BF), V((4, 2, 2, *block), BF),
        V((2, 2, *block), BF), V((2, 2, *block), BF), V((2, 2, 2, *block), BF), V((2, 2, 2, *block), BF),
        V((planes - 1, *block), BF), V((planes - 1, *block), BF),
        pltpu.SemaphoreType.DMA((n_sems,)), pltpu.SemaphoreType.DMA((n_sems,)),
        pltpu.SemaphoreType.DMA((members + 2,)),
    ]
    S = jax.ShapeDtypeStruct
    shapes = [
        ((1, points, width), BF), ((rows, width), F32), ((1, width), F32),
        ((vars_, width), F32), ((1, vars_), F32), ((1, 1), F32),
    ]
    held = pl.pallas_call(
        functools.partial(head_kernel, members, planes),
        out_shape=[pltpu.VMEM(*s) for s in shapes],
        in_specs=[hbm, vmem, vmem, vmem, vmem, hbm, vmem],
        out_specs=[vmem] * len(shapes),
        scratch_shapes=scratch,
        compiler_params=pltpu.CompilerParams(
            collective_id=0, has_side_effects=True, vmem_limit_bytes=55 * 1024 * 1024
        ),
    )(latent, w_in, b_in[None], w_out, b_out[None], targets, var_weight[None])
    gh, g_w1, g_b1, g_w2, g_b2, g_loss = pl.pallas_call(
        store_kernel,
        out_shape=[S(*s) for s in shapes],
        in_specs=[hbm] * len(shapes),
        out_specs=[hbm] * len(shapes),
        scratch_shapes=[pltpu.SemaphoreType.DMA((len(shapes),))],
        compiler_params=pltpu.CompilerParams(has_side_effects=True, vmem_limit_bytes=1024 * 1024),
    )(*[pltpu.with_memory_space_constraint(h, pltpu.VMEM) for h in held])
    return g_loss[0, 0], gh, g_w1, g_b1[0], g_w2, g_b2[0]


def local(latent, w_in, b_in, w_out, b_out, targets, var_weight, plan):
    members = lax.axis_size("member")
    grid = lax.axis_size("grid")
    points, width = latent.shape[1], latent.shape[2]
    whole_plan = plan.shape[0] == members - 1
    tiled = (
        w_in.shape[0] % 16 == 0 and grid == 8 and members == 4
        and points % (members * TILE) == 0 and width % (2 * members * LANES) == 0
        and width // members == grid * w_in.shape[0] and w_out.shape[0] < LANES
        and points * width <= 2048 * 1024
    )
    run = fast if whole_plan and tiled else shards
    return run(latent, w_in, b_in, w_out, b_out, targets, var_weight, plan)


def solution(mesh):
    placed = (
        P("member", "grid", None),
        P(("member", "grid"), None),
        P(),
        P(),
        P(),
        P(None, "grid"),
        P(),
        P(),
    )
    return jax.shard_map(
        local,
        mesh=mesh,
        in_specs=placed,
        out_specs=(P(), P("member", "grid", None), P(("member", "grid"), None), P(), P(), P()),
        check_vma=False,
    )
```

time: 90.6 us -> 68.4 us (0.75)
  Pallas kernels: 80.7 us -> 67.4 us
  local copies, waits for them, and re-layouts: 7.23 us -> 0 us
  between operations: 2.5 us -> 0.82 us
    pallas_call x1, Pallas kernels: 80.7 us -> 64.5 us  [fast(): pl.pallas_call(functools.partial(head_kernel, members, planes), out_shape...]
    unnamed x13 -> x0, local copies, waits for them, and re-layouts: 7.23 us -> none
    pallas_call x0 -> x1, Pallas kernels: none -> 2.87 us  [fast(): pl.pallas_call(store_kernel, out_shape=[S(*s) for s in shapes], in_specs=...]
where the time goes in v1:
time: 68.4 us; the launch traced here: 68.2 us
  Pallas kernels  67.4 us (99%)
  between operations  0.82 us (1%)
    pallas_call x1, Pallas kernels, fast(): pl.pallas_call(functools.partial(head_kernel, members, planes), out_shape...  64.5 us
    pallas_call x1, Pallas kernels, fast(): pl.pallas_call(store_kernel, out_shape=[S(*s) for s in shapes], in_specs=...  2.87 us

profile of v1, /device:TPU:0, one launch (start us, length us, event | category | flops | bytes accessed | tf_op | source)
XLA Modules:
  0.0 68.2 jit_solution(11247262719072060629)
XLA Ops:
  0.6 64.5 %shard_map.118 = (bf16[1,2048,1024]{2,1,0:T(8,128)(2,1)S(1)}, f32[32,1024]{1,0:T(8,128)S(1)}, f32[1,1024]{1,0:T(1,128)S(1)}, f32[100,1024]{1,0:T(8,128)S(1)}, f32[1,100]{1,0:T(1,128)S(1)}, /*index=5*/f32[1,1]{1,0:T(1,128)}) custom-call(bf16[1,2048,1024]{2,1,0:T(8,128)(2,1)} %lat_hbm.1, bf16[32,1024]{1,0:T(8,128)(2,1)} %w_in.1, f32[1,1024]{1,0:T(1,128)} %bitcast.6, ...), custom_call_target="tpu_custom_call" | custom-call | tf_op jit(solution)/shard_map/pallas_call | solution.py:556
  65.2 2.9 %shard_map.119 = (bf16[1,2048,1024]{2,1,0:T(8,128)(2,1)}, f32[32,1024]{1,0:T(8,128)}, f32[1,1024]{1,0:T(1,128)}, f32[100,1024]{1,0:T(8,128)}, f32[1,100]{1,0:T(1,128)}, /*index=5*/f32[1,1]{1,0:T(1,128)}) custom-call(bf16[1,2048,1024]{2,1,0:T(8,128)(2,1)S(1)} %get-tuple-element.18.refs_0_, f32[32,1024]{1,0:T(8,128)S(1)} %get-tuple-element.19.refs_1_, ...), custom_call_target="tpu_custom_call" | custom-call | tf_op jit(solution)/shard_map/pallas_call | solution.py:566

commit v2 on v1

--- a/solution.py
+++ b/solution.py
@@ -103,9 +103,9 @@
 
 
 def head_kernel(
-    members, planes, lat_hbm, w_in, b_in, w_out, b_out, tgt_hbm, vw,
+    members, planes, lat_hbm, w_in, b_in_hbm, w_out_hbm, b_out_hbm, tgt_hbm, vw_hbm,
     gh, g_w1, g_b1, g_w2, g_b2, g_loss,
-    lat, lat_t, w_buf, gp, act, dpre, wo, fown, fsend, frecv, csend, crecv, tgt, rowbuf, lane_sums,
+    lat, lat_t, w_buf, gp, act, dpre, b_in, w_out, b_out, vw, wo, fown, fsend, frecv, csend, crecv, tgt, rowbuf, lane_sums,
     ot, op_send, op_recv, om, om_send, om_recv, oq, w2, sm, sp_recv, smm, smz,
     keep, part_sum, p_send, p_recv, d_send, d_recv, n_send, n_recv, z_send, z_recv,
     send_sem, recv_sem, local_sem,
@@ -147,6 +147,80 @@
         started.append(copy)
         return copy
 
+    barrier = pltpu.get_barrier_semaphore()
+    peers = [partner] + [z_dev(k) for k in range(1, planes)] + [member_dev(s) for s in (DIAG, ACROSS, DOWN)]
+    for dev in peers:
+        pl.semaphore_signal(barrier, inc=1, device_id=dev, device_id_type=pl.DeviceIdType.MESH)
+    pl.semaphore_wait(barrier, len(peers))
+
+    near = {ACROSS: [], DOWN: []}
+    far = []
+    to_part = {s: [] for s in range(members)}
+    z_copies = [None]
+
+    def block(s, step):
+        return w_buf.at[mem[s], zed[step], c]
+
+    def hand_over(s, step):
+        to_part[s].append(send(block(s, step), block(s, step), partner))
+
+    def spread_block(step):
+        if step > 0:
+            z_copies[step].wait_recv()
+        if step == 2:
+            z_copies.append(send(block(SELF, 2), block(SELF, 2), z_dev(1)))
+        src = w_in if step == 0 else block(SELF, step)
+        for s in (ACROSS, DOWN):
+            near[s].append(send(src, block(SELF, step), member_dev(s)))
+        to_part[SELF].append(send(src, block(SELF, step), partner))
+
+    def relay_block(step):
+        for s in (ACROSS, DOWN):
+            near[s][step].wait_recv()
+        s = ACROSS if step % 2 == 0 else DOWN
+        far.append(send(block(s, step), block(s, step), member_dev(ACROSS + DOWN - s)))
+        hand_over(ACROSS, step)
+        hand_over(DOWN, step)
+
+    def far_block(step):
+        far[step].wait_recv()
+        hand_over(DIAG, step)
+
+    def transpose_next():
+        s, copy = loads.pop(0)
+        copy.wait()
+
+        def body(t, carry):
+            r0 = pl.multiple_of(t * 2 * TILE, 2 * TILE)
+            turned = lat[s, pl.ds(r0, 2 * TILE), :].T
+            lat_t[0, s, :, pl.ds(r0, 2 * TILE)] = turned[:half]
+            lat_t[1, s, :, pl.ds(r0, 2 * TILE)] = turned[half:]
+            return carry
+
+        lax.fori_loop(0, points // (2 * TILE), body, 0)
+
+    def contract(slots, first):
+        for s in slots:
+            for copy in to_part[s]:
+                copy.wait_recv()
+        big = 4 * TILE
+
+        def body(t, carry):
+            r0 = pl.multiple_of(t * big, big)
+            acc = b_in[...] if first else gp[pl.ds(r0, big), :]
+            for s in slots:
+                acc = acc + dot(lat[s, pl.ds(r0, big), :], w_buf[mem[s]].reshape(width, latent), NN)
+            gp[pl.ds(r0, big), :] = acc
+            return carry
+
+        lax.fori_loop(0, points // big, body, 0)
+
+    z_copies.append(send(w_in, w_buf.at[m, z, c], z_dev(1)))
+    z_copies.append(send(w_in, w_buf.at[m, z, c], z_dev(2)))
+    spread_block(0)
+
+    own = pltpu.make_async_copy(w_in, w_buf.at[m, z, c], local_sem.at[members])
+    own.start()
     loads = []
     for s in (SELF, ACROSS, DOWN, DIAG):
         copy = pltpu.make_async_copy(
@@ -154,84 +228,20 @@
         )
         copy.start()
         loads.append((s, copy))
-    own = pltpu.make_async_copy(w_in, w_buf.at[m, z, c], local_sem.at[members])
-    own.start()
     tgt_copy = pltpu.make_async_copy(
         tgt_hbm.at[:, pl.ds(pl.multiple_of(m * sub, LANES), sub)], tgt, local_sem.at[members + 1]
     )
     tgt_copy.start()
-
-    barrier = pltpu.get_barrier_semaphore()
-    peers = [partner] + [z_dev(k) for k in range(1, planes)] + [member_dev(s) for s in (DIAG, ACROSS, DOWN)]
-    for dev in peers:
-        pl.semaphore_signal(barrier, inc=1, device_id=dev, device_id_type=pl.DeviceIdType.MESH)
-    pl.semaphore_wait(barrier, len(peers))
-
-    near = {ACROSS: [], DOWN: []}
-    far = []
-    to_part = {s: [] for s in range(members)}
-    z_copies = [None]
-
-    def block(s, step):
-        return w_buf.at[mem[s], zed[step], c]
-
-    def hand_over(s, step):
-        to_part[s].append(send(block(s, step), block(s, step), partner))
-
-    def spread_block(step):
-        if step > 0:
-            z_copies[step].wait_recv()
-        src = w_in if step == 0 else block(SELF, step)
-        for s in (ACROSS, DOWN):
-            near[s].append(send(src, block(SELF, step), member_dev(s)))
-        to_part[SELF].append(send(src, block(SELF, step), partner))
-
-    def relay_block(step):
-        for s in (ACROSS, DOWN):
-            near[s][step].wait_recv()
-        s = ACROSS if step % 2 == 0 else DOWN
-        far.append(send(block(s, step), block(s, step), member_dev(ACROSS + DOWN - s)))
-        hand_over(ACROSS, step)
-        hand_over(DOWN, step)
-
-    def far_block(step):
-        far[step].wait_recv()
-        hand_over(DIAG, step)
-
-    def transpose_next():
-        s, copy = loads.pop(0)
+    small_copies = []
+    for n, (src, dst) in enumerate(((b_out_hbm, b_out), (vw_hbm, vw), (w_out_hbm, w_out), (b_in_hbm, b_in))):
+        copy = pltpu.make_async_copy(src, dst, local_sem.at[members + 2 + n])
+        copy.start()
+        small_copies.append(copy)
+
+
+    wo[...] = jnp.zeros_like(wo)
+    for copy in small_copies:
         copy.wait()
-
-        def body(t, carry):
-            r0 = pl.multiple_of(t * 2 * TILE, 2 * TILE)
-            turned = lat[s, pl.ds(r0, 2 * TILE), :].T
-            lat_t[0, s, :, pl.ds(r0, 2 * TILE)] = turned[:half]
-            lat_t[1, s, :, pl.ds(r0, 2 * TILE)] = turned[half:]
-            return carry
-
-        lax.fori_loop(0, points // (2 * TILE), body, 0)
-
-    def contract(slots, first):
-        for s in slots:
-            for copy in to_part[s]:
-                copy.wait_recv()
-        big = 4 * TILE
-
-        def body(t, carry):
-            r0 = pl.multiple_of(t * big, big)
-            acc = b_in[...] if first else gp[pl.ds(r0, big), :]
-            for s in slots:
-                acc = acc + dot(lat[s, pl.ds(r0, big), :], w_buf[mem[s]].reshape(width, latent), NN)
-            gp[pl.ds(r0, big), :] = acc
-            return carry
-
-        lax.fori_loop(0, points // big, body, 0)
-
-    for k in range(1, planes):
-        z_copies.append(send(w_in, w_buf.at[m, z, c], z_dev(k)))
-    spread_block(0)
-
-    wo[...] = jnp.zeros_like(wo)
     wo[:vars_, :] = w_out[...]
     rowbuf[...] = jnp.zeros_like(rowbuf)
     rowbuf[0:1, :vars_] = b_out[...]
@@ -241,6 +251,7 @@
     lane_sums[...] = jnp.zeros_like(lane_sums)
     ot[...] = jnp.zeros_like(ot)
     sm[...] = jnp.zeros_like(sm)
+    csend[...] = jnp.zeros_like(csend)
     own.wait()
 
     transpose_next()
@@ -270,16 +281,20 @@
     c_copies = {}
     sums = {"b": jnp.zeros((vars_, LANES), F32), "l": jnp.zeros((vars_, LANES), F32)}
 
-    def forward_tile(part, s):
+    def activate(part, s):
         r0 = pl.multiple_of(mem[s] * sub + part * TILE, TILE)
         x = dot(lat[DIAG, pl.ds(r0, TILE), :], w_buf[mem[DIAG]].reshape(width, latent), NN)
         x = x + gp[pl.ds(r0, TILE), :]
         sq = x * x
         cdf = 0.5 + 0.5 * jnp.tanh(x * (c0 + (0.044715 * c0) * sq))
         out = x * cdf
-        act[pl.ds(r0, TILE), :] = out.astype(BF)
+        rounded = out.astype(BF)
+        act[pl.ds(r0, TILE), :] = rounded
         gp[pl.ds(r0, TILE), :] = cdf + (out * (1.0 - cdf)) * (2.0 * c0 + (6.0 * 0.044715 * c0) * sq)
-        field = dot(wo[...], act[pl.ds(r0, TILE), :], NT)
+        return rounded
+
+    def project(part, s, rounded):
+        field = dot(wo[...], rounded, NT)
         if s == SELF:
             fown[part] = field[:vars_]
         else:
@@ -290,6 +305,9 @@
             at = lax.broadcasted_iota(jnp.int32, (pad, TILE), 0)
             coded = jnp.where(at == vars_, jnp.broadcast_to(code, (pad, TILE)), coded)
             fsend[part, s] = coded.astype(jnp.int32).astype(I16)
+
+    def send_field(part, s):
+        if s != SELF:
             f_copies[part, s] = send(fsend.at[part, s], frecv.at[part, s], member_dev(s))
 
     def score(part):
@@ -329,21 +347,24 @@
                 cot = scale * (d * inv - pairs[s] * (1.0 / (members - 1)))
                 b_sum += cot
                 if s == SELF:
-                    crecv[part, SELF, :, cols] = cot.astype(BF)
+                    crecv[part, SELF, :vars_, cols] = cot.astype(BF)
                 else:
-                    csend[part, s, :, cols] = cot.astype(BF)
+                    csend[part, s, :vars_, cols] = cot.astype(BF)
             l_sum += scale * (miss_sum - spread * (1.0 / (members - 1)))
         sums["b"], sums["l"] = b_sum, l_sum
         for s in (DIAG, ACROSS, DOWN):
             c_copies[part, s] = send(csend.at[part, s], crecv.at[part, s], member_dev(s))
 
     tgt_copy.wait()
-    for part in range(parts):
-        for s in (DIAG, ACROSS, DOWN):
-            forward_tile(part, s)
-        if part > 0:
+    todo = [(part, s) for part in range(parts) for s in (DIAG, ACROSS, DOWN, SELF)]
+    ready = activate(*todo[0])
+    for n, (part, s) in enumerate(todo):
+        project(part, s, ready)
+        if n + 1 < len(todo):
+            ready = activate(*todo[n + 1])
+        send_field(part, s)
+        if s == DOWN and part > 0:
             score(part - 1)
-        forward_tile(part, SELF)
     score(parts - 1)
     lane_sums[:vars_, :] = sums["b"]
     sm[1:2, :LANES] = jnp.sum(lane_sums[...].T, axis=0, keepdims=True)
@@ -352,10 +373,11 @@
     col = jnp.zeros((1, latent), F32)
     for part in range(parts):
         for s in (SELF, ACROSS, DOWN, DIAG):
-            if s != SELF:
-                c_copies[part, s].wait_recv()
+            if s == ACROSS:
+                for k in (ACROSS, DOWN, DIAG):
+                    c_copies[part, k].wait_recv()
             r0 = pl.multiple_of(mem[s] * sub + part * TILE, TILE)
-            cot_b = crecv[part, s]
+            cot_b = crecv[part, s, :vars_]
             d = dot(cot_b, w_out[...], TN) * gp[pl.ds(r0, TILE), :]
             dpre[pl.ds(r0, TILE), :] = d.astype(BF)
             ot[:vars_, :] += dot(cot_b, act[pl.ds(r0, TILE), :], NN)
@@ -395,13 +417,15 @@
                 send(d_send.at[h, j], d_recv.at[h, j], member_dev(ACROSS + j)) for j in range(2)
             ]
             n_send[h, 0, 0] = both[1, 0].astype(BF)
-            n_copies[h, ACROSS, 0] = send(n_send.at[h, 0, 0], n_recv.at[h, 0, 0], member_dev(ACROSS))
             part_sum[h, ACROSS, 1] = both[1, 1]
         else:
             n_send[h, 1, 1] = both[0, 1].astype(BF)
-            n_copies[h, DOWN, 1] = send(n_send.at[h, 1, 1], n_recv.at[h, 1, 1], member_dev(DOWN))
             part_sum[h, DOWN, 0] = both[0, 0]
             part_sum[h, SELF] = both[1]
+
+    def direct(h, s):
+        j = s - 1
+        n_copies[h, s, j] = send(n_send.at[h, j, j], n_recv.at[h, j, j], member_dev(s))
 
     def relay_sum(h):
         for s, j in ((DOWN, 0), (ACROSS, 1)):
@@ -416,42 +440,59 @@
         part_sum[h, SELF] = (part_sum[h, SELF] + n_recv[h, 0].astype(F32)) + n_recv[h, 1].astype(F32)
 
     side = lax.rem(z, 2)
-    zz_copies = {}
-
-    def to_plane(k):
-        h = 0 if k > 1 else 1
-        j = side if k == 2 else 1 - side
-        z_send[k - 1] = part_sum[h, SELF, j].astype(BF)
-        zz_copies[k] = send(z_send.at[k - 1], z_recv.at[k - 1], z_dev(k))
+    zz_copies = []
+
+    def to_plane(n, value, k):
+        z_send[n] = value.astype(BF)
+        zz_copies.append(send(z_send.at[n], z_recv.at[n], z_dev(k)))
 
     def hidden_grad(ch):
         w = w_buf[ch].reshape(width, latent)
         gh[0, :, ch * width:(ch + 1) * width] = dot(dpre[...], w, NT).astype(BF)
 
+    def open_out():
+        op_copy.wait_recv()
+        mine = pl.multiple_of(c * (planes * share), share)
+        om[...] = (ot[pl.ds(mine, planes * share), :] + op_recv[...].astype(F32)).reshape(planes, share, latent)
+        om_send[...] = om[...].astype(BF)
+        return [send(om_send.at[zed[k]], om_recv.at[k - 1], z_dev(k)) for k in range(1, planes)]
+
+    def cross_out():
+        acc = om[z]
+        for k in range(1, planes):
+            om_copies[k - 1].wait_recv()
+            acc += om_recv[k - 1].astype(F32)
+        oq[m] = acc.astype(BF)
+        return [send(oq.at[m], oq.at[m], member_dev(s)) for s in (DIAG, ACROSS, DOWN)]
+
+    def close_out():
+        for copy in oq_copies:
+            copy.wait_recv()
+        acc = oq[0].astype(F32)
+        for k in range(1, members):
+            acc += oq[k].astype(F32)
+        w2[c, z] = acc.astype(BF)
+        return [send(w2.at[c, z], w2.at[c, z], z_dev(k)) for k in range(1, planes)]
+
     chunk(0, 0)
-    chunk(0, 1)
-    fold(0, 0)
-    chunk(1, 0)
-    fold(0, 1)
-    op_copy.wait_recv()
-    mine = pl.multiple_of(c * (planes * share), share)
-    om[...] = (ot[pl.ds(mine, planes * share), :] + op_recv[...].astype(F32)).reshape(planes, share, latent)
-    om_send[...] = om[...].astype(BF)
-    om_copies = [send(om_send.at[zed[k]], om_recv.at[k - 1], z_dev(k)) for k in range(1, planes)]
+    om_copies = open_out()
     sp_copy.wait_recv()
     smm[m] = sm[...] + sp_recv[...]
     sm_copies = [send(smm.at[m], smm.at[m], member_dev(s)) for s in (DIAG, ACROSS, DOWN)]
+    chunk(0, 1)
+    fold(0, 0)
+    direct(0, ACROSS)
+    chunk(1, 0)
+    fold(0, 1)
+    direct(0, DOWN)
     chunk(1, 1)
+    oq_copies = cross_out()
     relay_sum(0)
+    hidden_grad(0)
     fold(1, 0)
+    direct(1, ACROSS)
     fold(1, 1)
-    hidden_grad(0)
-    acc = om[z]
-    for k in range(1, planes):
-        om_copies[k - 1].wait_recv()
-        acc += om_recv[k - 1].astype(F32)
-    oq[m] = acc.astype(BF)
-    oq_copies = [send(oq.at[m], oq.at[m], member_dev(s)) for s in (DIAG, ACROSS, DOWN)]
+    direct(1, DOWN)
     for copy in sm_copies:
         copy.wait_recv()
     acc = smm[0]
@@ -459,45 +500,38 @@
         acc += smm[k]
     smz[z] = acc
     sz_copies = [send(smz.at[z], smz.at[z], z_dev(k)) for k in range(1, planes)]
+    w2_copies = close_out()
+    hidden_grad(1)
     plane_sum(0)
-    to_plane(2)
-    to_plane(3)
-    hidden_grad(1)
+    to_plane(0, part_sum[0, SELF, 1 - side], 1)
+    hidden_grad(2)
     relay_sum(1)
-    hidden_grad(2)
-    for copy in oq_copies:
+    zz_copies[0].wait_recv()
+    to_plane(1, part_sum[0, SELF, side] + z_recv[0].astype(F32), 2)
+    hidden_grad(3)
+    for copy in w2_copies:
         copy.wait_recv()
-    acc = oq[0].astype(F32)
-    for k in range(1, members):
-        acc += oq[k].astype(F32)
-    w2[c, z] = acc.astype(BF)
-    w2_copies = [send(w2.at[c, z], w2.at[c, z], z_dev(k)) for k in range(1, planes)]
-    hidden_grad(3)
+    half_copy = send(w2.at[c], w2.at[c], partner)
     plane_sum(1)
-    to_plane(1)
-    part_sum[1, SELF, 0] = part_sum[1, SELF, side]
+    to_plane(2, part_sum[1, SELF, 1 - side], 1)
+    acc = part_sum[1, SELF, side]
 
     kappa = 4.0 / math.sqrt(members * total)
     for copy in sz_copies:
         copy.wait_recv()
-    acc = smz[0]
+    small = smz[0]
     for k in range(1, planes):
-        acc += smz[k]
-    acc = acc * kappa
-    g_b1[...] = acc[0:1, :]
-    g_b2[...] = acc[1:2, :vars_]
-    g_loss[...] = jnp.sum(acc[1:2, LANES:2 * LANES], axis=1, keepdims=True) * (1.0 / (kappa * members * total * vars_))
-    for copy in w2_copies:
-        copy.wait_recv()
-    half_copy = send(w2.at[c], w2.at[c], partner)
-
-    acc = part_sum[1, SELF, 0]
-    for k in (2, 3, 1):
-        zz_copies[k].wait_recv()
-        acc += z_recv[k - 1].astype(F32)
-    g_w1[...] = acc * kappa
+        small += smz[k]
+    small = small * kappa
+    g_b1[...] = small[0:1, :]
+    g_b2[...] = small[1:2, :vars_]
+    g_loss[...] = jnp.sum(small[1:2, LANES:2 * LANES], axis=1, keepdims=True) * (1.0 / (kappa * members * total * vars_))
     half_copy.wait_recv()
     g_w2[...] = w2[...].reshape(2 * planes * share, latent)[:vars_].astype(F32) * kappa
+    for n in (1, 2):
+        zz_copies[n].wait_recv()
+        acc += z_recv[n].astype(F32)
+    g_w1[...] = acc * kappa
     for copy in started:
         copy.wait_send()
 
@@ -533,9 +567,10 @@
     scratch = [
         V((members, points, cw), BF), V((2, members, cw // 2, points), BF), V((members, planes, 2, *block), BF),
         V((points, width), F32), V((points, width), BF), V((points, width), BF),
+        V((1, width), F32), V((vars_, width), BF), V((1, vars_), F32), V((1, vars_), F32),
         V((pad, width), BF), V((parts, vars_, TILE), F32),
         V((parts, members - 1, pad, TILE), I16), V((parts, members - 1, pad, TILE), I16),
-        V((parts, members - 1, vars_, TILE), BF), V((parts, members, vars_, TILE), BF), V((vars_, sub), F32),
+        V((parts, members - 1, pad, TILE), BF), V((parts, members, pad, TILE), BF), V((vars_, sub), F32),
         V((8, LANES), F32), V((LANES, LANES), F32),
         V((2 * planes * share, width), F32), V((planes * share, width), BF), V((planes * share, width), BF),
         V((planes, share, width), F32), V((planes, share, width), BF), V((planes - 1, share, width), BF),
@@ -546,7 +581,7 @@
         V((2, 2, *block), BF), V((2, 2, *block), BF), V((2, 2, 2, *block), BF), V((2, 2, 2, *block), BF),
         V((planes - 1, *block), BF), V((planes - 1, *block), BF),
         pltpu.SemaphoreType.DMA((n_sems,)), pltpu.SemaphoreType.DMA((n_sems,)),
-        pltpu.SemaphoreType.DMA((members + 2,)),
+        pltpu.SemaphoreType.DMA((members + 6,)),
     ]
     S = jax.ShapeDtypeStruct
     shapes = [
@@ -556,11 +591,11 @@
     held = pl.pallas_call(
         functools.partial(head_kernel, members, planes),
         out_shape=[pltpu.VMEM(*s) for s in shapes],
-        in_specs=[hbm, vmem, vmem, vmem, vmem, hbm, vmem],
+        in_specs=[hbm] * 7,
         out_specs=[vmem] * len(shapes),
         scratch_shapes=scratch,
         compiler_params=pltpu.CompilerParams(
-            collective_id=0, has_side_effects=True, vmem_limit_bytes=55 * 1024 * 1024
+            collective_id=0, has_side_effects=True, vmem_limit_bytes=57000 * 1024
         ),
     )(latent, w_in, b_in[None], w_out, b_out[None], targets, var_weight[None])
     gh, g_w1, g_b1, g_w2, g_b2, g_loss = pl.pallas_call(

time: 68.4 us -> 66.1 us (0.966)
  Pallas kernels: 67.4 us -> 65.1 us
    pallas_call x1, Pallas kernels: 64.5 us -> 62.2 us  [fast(): pl.pallas_call(functools.partial(head_kernel, members, planes), out_shape...]
where the time goes in v2:
time: 66.1 us; the launch traced here: 65.9 us
  Pallas kernels  65.1 us (98%)
  between operations  0.82 us (1%)
    pallas_call x1, Pallas kernels, fast(): pl.pallas_call(functools.partial(head_kernel, members, planes), out_shape...  62.2 us
    pallas_call x1, Pallas kernels, fast(): pl.pallas_call(store_kernel, out_shape=[S(*s) for s in shapes], in_specs=...  2.87 us

profile of v2, /device:TPU:0, one launch (start us, length us, event | category | flops | bytes accessed | tf_op | source)
XLA Modules:
  0.0 65.9 jit_solution(1164870225635009699)
XLA Ops:
  0.6 62.2 %shard_map.118 = (bf16[1,2048,1024]{2,1,0:T(8,128)(2,1)S(1)}, f32[32,1024]{1,0:T(8,128)S(1)}, f32[1,1024]{1,0:T(1,128)S(1)}, f32[100,1024]{1,0:T(8,128)S(1)}, f32[1,100]{1,0:T(1,128)S(1)}, /*index=5*/f32[1,1]{1,0:T(1,128)}) custom-call(bf16[1,2048,1024]{2,1,0:T(8,128)(2,1)} %lat_hbm.1, bf16[32,1024]{1,0:T(8,128)(2,1)} %w_in.1, f32[1,1024]{1,0:T(1,128)} %bitcast.6, ...), custom_call_target="tpu_custom_call" | custom-call | tf_op jit(solution)/shard_map/pallas_call | solution.py:591
  62.9 2.9 %shard_map.119 = (bf16[1,2048,1024]{2,1,0:T(8,128)(2,1)}, f32[32,1024]{1,0:T(8,128)}, f32[1,1024]{1,0:T(1,128)}, f32[100,1024]{1,0:T(8,128)}, f32[1,100]{1,0:T(1,128)}, /*index=5*/f32[1,1]{1,0:T(1,128)}) custom-call(bf16[1,2048,1024]{2,1,0:T(8,128)(2,1)S(1)} %get-tuple-element.18.refs_0_, f32[32,1024]{1,0:T(8,128)S(1)} %get-tuple-element.19.refs_1_, ...), custom_call_target="tpu_custom_call" | custom-call | tf_op jit(solution)/shard_map/pallas_call | solution.py:601

commit v3 on v2

--- a/solution.py
+++ b/solution.py
@@ -504,16 +504,16 @@
     hidden_grad(1)
     plane_sum(0)
     to_plane(0, part_sum[0, SELF, 1 - side], 1)
+    relay_sum(1)
     hidden_grad(2)
-    relay_sum(1)
     zz_copies[0].wait_recv()
     to_plane(1, part_sum[0, SELF, side] + z_recv[0].astype(F32), 2)
-    hidden_grad(3)
     for copy in w2_copies:
         copy.wait_recv()
     half_copy = send(w2.at[c], w2.at[c], partner)
     plane_sum(1)
     to_plane(2, part_sum[1, SELF, 1 - side], 1)
+    hidden_grad(3)
     acc = part_sum[1, SELF, side]
 
     kappa = 4.0 / math.sqrt(members * total)

time: 66.1 us -> 64.7 us (0.979)
  Pallas kernels: 65.1 us -> 63.7 us
    pallas_call x1, Pallas kernels: 62.2 us -> 60.9 us  [fast(): pl.pallas_call(functools.partial(head_kernel, members, planes), out_shape...]
where the time goes in v3:
time: 64.7 us; the launch traced here: 64.6 us
  Pallas kernels  63.7 us (98%)
  between operations  0.82 us (1%)
    pallas_call x1, Pallas kernels, fast(): pl.pallas_call(functools.partial(head_kernel, members, planes), out_shape...  60.9 us
    pallas_call x1, Pallas kernels, fast(): pl.pallas_call(store_kernel, out_shape=[S(*s) for s in shapes], in_specs=...  2.87 us

profile of v3, /device:TPU:0, one launch (start us, length us, event | category | flops | bytes accessed | tf_op | source)
XLA Modules:
  0.0 64.6 jit_solution(14481860317910859581)
XLA Ops:
  0.6 60.9 %shard_map.118 = (bf16[1,2048,1024]{2,1,0:T(8,128)(2,1)S(1)}, f32[32,1024]{1,0:T(8,128)S(1)}, f32[1,1024]{1,0:T(1,128)S(1)}, f32[100,1024]{1,0:T(8,128)S(1)}, f32[1,100]{1,0:T(1,128)S(1)}, /*index=5*/f32[1,1]{1,0:T(1,128)}) custom-call(bf16[1,2048,1024]{2,1,0:T(8,128)(2,1)} %lat_hbm.1, bf16[32,1024]{1,0:T(8,128)(2,1)} %w_in.1, f32[1,1024]{1,0:T(1,128)} %bitcast.6, ...), custom_call_target="tpu_custom_call" | custom-call | tf_op jit(solution)/shard_map/pallas_call | solution.py:591
  61.5 2.9 %shard_map.119 = (bf16[1,2048,1024]{2,1,0:T(8,128)(2,1)}, f32[32,1024]{1,0:T(8,128)}, f32[1,1024]{1,0:T(1,128)}, f32[100,1024]{1,0:T(8,128)}, f32[1,100]{1,0:T(1,128)}, /*index=5*/f32[1,1]{1,0:T(1,128)}) custom-call(bf16[1,2048,1024]{2,1,0:T(8,128)(2,1)S(1)} %get-tuple-element.18.refs_0_, f32[32,1024]{1,0:T(8,128)S(1)} %get-tuple-element.19.refs_1_, ...), custom_call_target="tpu_custom_call" | custom-call | tf_op jit(solution)/shard_map/pallas_call | solution.py:601

commit v4 on v3

--- a/solution.py
+++ b/solution.py
@@ -508,11 +508,11 @@
     hidden_grad(2)
     zz_copies[0].wait_recv()
     to_plane(1, part_sum[0, SELF, side] + z_recv[0].astype(F32), 2)
+    plane_sum(1)
+    to_plane(2, part_sum[1, SELF, 1 - side], 1)
     for copy in w2_copies:
         copy.wait_recv()
     half_copy = send(w2.at[c], w2.at[c], partner)
-    plane_sum(1)
-    to_plane(2, part_sum[1, SELF, 1 - side], 1)
     hidden_grad(3)
     acc = part_sum[1, SELF, side]
 

time: 64.7 us -> 64.7 us (level)
  no operation moved by 1% of the time
where the time goes in v4:
time: 64.7 us; the launch traced here: 64.6 us
  Pallas kernels  63.7 us (98%)
  between operations  0.82 us (1%)
    pallas_call x1, Pallas kernels, fast(): pl.pallas_call(functools.partial(head_kernel, members, planes), out_shape...  60.9 us
    pallas_call x1, Pallas kernels, fast(): pl.pallas_call(store_kernel, out_shape=[S(*s) for s in shapes], in_specs=...  2.87 us

profile of v4, /device:TPU:0, one launch (start us, length us, event | category | flops | bytes accessed | tf_op | source)
XLA Modules:
  0.0 64.6 jit_solution(3675743841088072344)
XLA Ops:
  0.6 60.9 %shard_map.118 = (bf16[1,2048,1024]{2,1,0:T(8,128)(2,1)S(1)}, f32[32,1024]{1,0:T(8,128)S(1)}, f32[1,1024]{1,0:T(1,128)S(1)}, f32[100,1024]{1,0:T(8,128)S(1)}, f32[1,100]{1,0:T(1,128)S(1)}, /*index=5*/f32[1,1]{1,0:T(1,128)}) custom-call(bf16[1,2048,1024]{2,1,0:T(8,128)(2,1)} %lat_hbm.1, bf16[32,1024]{1,0:T(8,128)(2,1)} %w_in.1, f32[1,1024]{1,0:T(1,128)} %bitcast.6, ...), custom_call_target="tpu_custom_call" | custom-call | tf_op jit(solution)/shard_map/pallas_call | solution.py:591
  61.5 2.9 %shard_map.119 = (bf16[1,2048,1024]{2,1,0:T(8,128)(2,1)}, f32[32,1024]{1,0:T(8,128)}, f32[1,1024]{1,0:T(1,128)}, f32[100,1024]{1,0:T(8,128)}, f32[1,100]{1,0:T(1,128)}, /*index=5*/f32[1,1]{1,0:T(1,128)}) custom-call(bf16[1,2048,1024]{2,1,0:T(8,128)(2,1)S(1)} %get-tuple-element.18.refs_0_, f32[32,1024]{1,0:T(8,128)S(1)} %get-tuple-element.19.refs_1_, ...), custom_call_target="tpu_custom_call" | custom-call | tf_op jit(solution)/shard_map/pallas_call | solution.py:601
